TPU v7x, 256 devices: a whole 4x4x8 slice. The times are simulated.
256 devices in a mesh: ket: 16 (over x, y_hi, core), bra: 16 (over z, y_lo).
Axes of the slice: x: 4, y: 4 (y_hi: 2, y_lo: 2; y = y_hi * 2 + y_lo), z: 8, core: 2. Of those that a mesh axis runs over, the one named last changes fastest.
Arguments:
- density: bfloat16 [2, 2, 12288, 12288], P(None, None, 'ket', 'bra'), may hold values from -6 to 6
- coupling: bfloat16 [48, 3, 256, 256], P('bra'), may hold values from -0.21875 to 0.21875
- block_cols: int32 [48, 3], replicated, may hold values from 0 to 47, as said below
- block_count: int32 [48], replicated, may hold values from 2 to 3, as said below
- energies: float32 [12288], replicated, may hold values from -0.5 to 97
Outputs:
- dissipated: bfloat16 [2, 2, 12288, 12288], P(None, None, 'ket', 'bra')
Inputs may be any that keep to these rules, and one draw needn't show every extreme that they name: Row i of block_cols holds i - 1, i and i + 1 in some order; entries that would lie outside 0 to 47 stand last and are replaced by i. Slots k < block_count[i] name distinct blocks. block_count[i] is at most the number of block columns of i - 1, i, i + 1 inside the grid.
All inputs are finite; a program needn't handle non-finite values.
Results may differ from a plain program's by a relative error of at most 0.0054.
Values may be sent and summed in bfloat16 or wider, within the bound.
A program may use at most 320 MiB of HBM per device.

v0:
```python
import jax
import jax.numpy as jnp
from jax import lax
from jax.sharding import PartitionSpec as P

thermal_beta_factor = 1.0
frequency_cutoff_scale = 4.0


def broadcast(value, axis, source):
    kept = jnp.where(lax.axis_index(axis) == source, value, 0).astype(value.dtype)
    return lax.psum(kept, axis)


def with_halo(block, sides, width):
    for axis, dim in sides:
        count = lax.axis_size(axis)
        forward = [(i, i + 1) for i in range(count - 1)]
        backward = [(target, source) for source, target in forward]
        low = lax.ppermute(
            lax.slice_in_dim(block, block.shape[dim] - width, None, axis=dim), axis, forward
        )
        high = lax.ppermute(lax.slice_in_dim(block, 0, width, axis=dim), axis, backward)
        block = jnp.concatenate([low, block, high], axis=dim)
    return block


def weigh(matrix, start_block, block_cols, block_count, energies):
    row_count = matrix.shape[0]
    slots = matrix.shape[1]
    block_size = matrix.shape[2]
    block_total = block_cols.shape[0]
    position = start_block + jnp.arange(row_count, dtype=jnp.int32)
    inside = (position >= 0) & (position < block_total)
    clamped = jnp.clip(position, 0, block_total - 1)
    columns = jnp.take(block_cols, clamped, axis=0)
    counts = jnp.take(block_count, clamped, axis=0)
    kept_levels = (jnp.arange(slots, dtype=jnp.int32)[None, :] < counts[:, None]) & inside[:, None]
    levels = energies.reshape(block_total, block_size)
    row_levels = jnp.take(levels, clamped, axis=0)
    col_levels = jnp.take(levels, columns.reshape(-1), axis=0).reshape(row_count, slots, block_size)
    energy_detuning = row_levels[:, None, :, None] - col_levels[:, :, None, :]
    spectral_density = jax.nn.sigmoid(thermal_beta_factor * energy_detuning) * jnp.exp(
        -jnp.abs(energy_detuning) / frequency_cutoff_scale
    )
    held = kept_levels[:, :, None, None]
    operator = jnp.where(held, matrix, jnp.zeros_like(matrix))
    weighted = jnp.where(
        held, matrix.astype(jnp.float32) * spectral_density, jnp.float32(0.0)
    ).astype(jnp.bfloat16)
    return (operator, weighted, columns)


def left_apply(matrix, columns, start_block, source_operator):
    copies, halves, source_rows, breadth = source_operator.shape
    row_count, slots, block_size = (matrix.shape[0], matrix.shape[1], matrix.shape[2])
    pieces = source_operator.reshape(copies, halves, source_rows // block_size, block_size, breadth)
    relative = (columns - start_block).reshape(-1)
    picked = jnp.take(pieces, relative, axis=2).reshape(
        copies, halves, row_count, slots, block_size, breadth
    )
    result = jnp.einsum("ikab,rpikbc->rpiac", matrix, picked, preferred_element_type=jnp.float32)
    return result.reshape(copies, halves, row_count * block_size, breadth)


def right_apply(matrix, columns, start_block, source_operator):
    copies, halves, source_rows, breadth = source_operator.shape
    row_count, slots, block_size = (matrix.shape[0], matrix.shape[1], matrix.shape[2])
    pieces = source_operator.reshape(copies, halves, source_rows, breadth // block_size, block_size)
    relative = (columns - start_block).reshape(-1)
    picked = jnp.take(pieces, relative, axis=3).reshape(
        copies, halves, source_rows, row_count, slots, block_size
    )
    result = jnp.einsum("rpxjkb,jkab->rpxja", picked, matrix, preferred_element_type=jnp.float32)
    return result.reshape(copies, halves, source_rows, row_count * block_size)


def body(density, coupling, block_cols, block_count, energies):
    block_size = coupling.shape[2]
    tile_rows = density.shape[2]
    tile_cols = density.shape[3]
    row_blocks = tile_rows // block_size
    col_blocks = tile_cols // block_size
    ket_index = lax.axis_index("ket")
    bra_index = lax.axis_index("bra")
    panel_owner = ket_index * lax.axis_size("bra") // lax.axis_size("ket")
    panel = broadcast(coupling, "bra", panel_owner)
    row_start = ket_index * row_blocks
    col_start = bra_index * col_blocks
    bordered = with_halo(density, (("ket", 2), ("bra", 3)), block_size)
    row_operator, row_weighted, row_columns = weigh(
        panel, row_start, block_cols, block_count, energies
    )
    col_operator, col_weighted, col_columns = weigh(
        coupling, col_start, block_cols, block_count, energies
    )
    commutand = (
        left_apply(
            row_weighted,
            row_columns,
            row_start - 1,
            bordered[:, :, :, block_size : block_size + tile_cols],
        )
        - right_apply(
            col_weighted,
            col_columns,
            col_start - 1,
            bordered[:, :, block_size : block_size + tile_rows, :],
        )
    ).astype(jnp.bfloat16)
    outer = with_halo(commutand, (("ket", 2), ("bra", 3)), block_size)
    dissipated = (
        right_apply(
            col_operator,
            col_columns,
            col_start - 1,
            outer[:, :, block_size : block_size + tile_rows, :],
        )
        - left_apply(
            row_operator,
            row_columns,
            row_start - 1,
            outer[:, :, :, block_size : block_size + tile_cols],
        )
    ).astype(jnp.bfloat16)
    return dissipated


def solution(mesh):
    return jax.shard_map(
        body,
        mesh=mesh,
        in_specs=(P(None, None, "ket", "bra"), P("bra", None, None, None), P(), P(), P()),
        out_specs=P(None, None, "ket", "bra"),
        check_vma=False,
    )
```

profile of v0, /device:TPU:92, one launch (start us, length us, event | category | flops | bytes accessed | tf_op | source)
XLA Modules:
  0.0 556.4 jit_solution(13479946788003193734)
XLA Ops:
  22.0 84.1 %collective-permute-done = bf16[2,2,256,768]{3,2,1,0:T(8,128)(2,1)} collective-permute-done((bf16[2,2,256,768]{3,2,1,0:T(8,128)(2,1)}, bf16[2,2,256,768]{3,2,1,0:T(8,128)(2,1)}, u32[]{:S(2)}, u32[]{:S(2)}) %collective-permute-start) | collective-permute-done | bytes 1572896 | tf_op jit(solution)/shard_map/ppermute | solution.py:20
  123.8 10.0 %gather_fusion.2 = bf16[9,2,2,256,768]{4,3,2,1,0:T(8,128)(2,1)} fusion(bf16[2,2,5,256,768]{4,3,1,0,2:T(8,128)(2,1)} %copy.31, s32[1024]{0:T(1024)S(1)} %get-tuple-element.25), kind=kCustom, calls=%fused_computation.2.clone | custom fusion | bytes 28311588 | tf_op jit(solution)/shard_map/jit(_take)/gather | solution.py:59
  133.9 10.7 %broadcast_select_fusion.3 = bf16[9,2,2,256,768]{4,3,2,1,0:T(8,128)(2,1)} fusion(bf16[9,2,2,256,768]{4,3,2,1,0:T(8,128)(2,1)} %gather_fusion.2, pred[9]{0:T(512)(128)(4,1)S(1)} %compare_and_fusion.3), kind=kLoop, calls=%fused_computation.15 | loop fusion | flops 7077888 | bytes 28311560 | tf_op jit(solution)/shard_map/jit(_take)/select_n | solution.py:59
  144.6 84.9 %all-reduce.2.cloned.1.call-done = bf16[3,3,256,256]{3,2,1,0:T(8,128)(2,1)} async-done(((bf16[3,3,256,256]{3,2,1,0:T(8,128)(2,1)}), bf16[3,3,256,256]{3,2,1,0:T(8,128)(2,1)}) %all-reduce.2.cloned.1.call-update) | async-done | bytes 1179664 | tf_op jit(solution)/shard_map/psum | solution.py:12
  229.5 9.1 %convolution_bitcast_fusion.3 = f32[2,2,3,256,768]{4,3,1,0,2:T(8,128)S(1)} fusion(bf16[2,2,3,3,256,768]{5,4,1,0,3,2:T(8,128)(2,1)} %bitcast.92, bf16[3,3,256,256]{3,2,1,0:T(8,128)(2,1)} %all-reduce.2.cloned.1.call-done, f32[3,3,256]{2,1,0:T(4,128)S(1)} %sub.69, f32[3,256]{1,0:T(4,128)S(1)} %broadcast_select_fusion.8, pred[3,3]{1,0:T(4,128)(4,1)S(1)} %fusion.47), kind=kOutput, calls=%fused_computation.30 | convolution fusion | flops 3630956544 | bytes 24784904 | tf_op jit(solution)/shard_map/ikab,rpikbc->rpiac/dot_general | solution.py:62
  238.6 4.8 copy.34
  243.4 6.7 %pad_maximum_fusion.4 = bf16[2,2,768,1280]{3,2,1,0:T(8,128)(2,1)} fusion(bf16[2,2,1280,256]{3,2,1,0:T(8,128)(2,1)} %collective-permute-done.3, bf16[2,2,1280,768]{3,2,1,0:T(8,128)(2,1)} %copy-done.3, bf16[2,2,1280,256]{3,2,1,0:T(8,128)(2,1)} %collective-permute-done.2), kind=kLoop, calls=%fused_computation.24 | loop fusion | flops 23592960 | bytes 20971520 | tf_op jit(solution)/shard_map/concatenate | solution.py:24
  250.1 10.7 %copy.35 = bf16[2,2,768,1280]{2,3,1,0:T(8,128)(2,1)} copy(bf16[2,2,768,1280]{3,2,1,0:T(8,128)(2,1)} %pad_maximum_fusion.4) | data formatting | bytes 15728640 | tf_op jit(solution)/shard_map/slice | solution.py:108
  260.7 7.1 %copy.36 = bf16[2,2,768,5,256]{2,4,1,0,3:T(8,128)(2,1)} copy(bf16[2,2,768,5,256]{2,4,3,1,0:T(8,128)(2,1)} %bitcast.90) | data formatting | bytes 15728640 | tf_op jit(solution)/shard_map/reshape | solution.py:69
  267.8 10.0 %gather_fusion.9 = bf16[9,2,2,768,256]{3,4,2,1,0:T(8,128)(2,1)} fusion(bf16[2,2,768,5,256]{2,4,1,0,3:T(8,128)(2,1)} %copy.36, s32[1024]{0:T(1024)S(1)} %pad_clamp_fusion), kind=kCustom, calls=%fused_computation.5.clone | custom fusion | bytes 28311588 | tf_op jit(solution)/shard_map/jit(_take)/gather | solution.py:71
  277.8 7.1 %broadcast_select_fusion = bf16[9,2,2,768,256]{3,4,2,1,0:T(8,128)(2,1)S(1)} fusion(bf16[9,2,2,768,256]{3,4,2,1,0:T(8,128)(2,1)} %gather_fusion.9, pred[9]{0:T(512)(128)(4,1)S(1)} %compare_and_fusion), kind=kLoop, calls=%fused_computation.12 | loop fusion | flops 7077888 | bytes 28311560 | tf_op jit(solution)/shard_map/jit(_take)/select_n | solution.py:71
  284.9 4.5 convolution_bitcast_fusion.2
  289.4 4.7 copy.39
  294.1 9.7 %copy.40 = f32[2,2,768,768]{3,2,1,0:T(8,128)} copy(f32[2,2,768,768]{2,3,1,0:T(8,128)} %bitcast.88) | data formatting | bytes 18874368 | tf_op jit(solution)/shard_map/reshape | solution.py:75
  303.8 10.1 %fusion.1 = bf16[2,2,768,768]{3,2,1,0:T(8,128)(2,1)} fusion(f32[2,2,768,768]{3,2,1,0:T(8,128)} %copy.40, f32[2,2,3,256,768]{4,3,2,1,0:T(8,128)} %copy.34), kind=kLoop, calls=%fused_computation.19 | loop fusion | flops 4718592 | bytes 23592960 | tf_op jit(solution)/shard_map/convert_element_type | solution.py:110
  318.2 5.1 collective-permute-start.5
  323.4 89.7 %collective-permute-done.4 = bf16[2,2,256,768]{3,2,1,0:T(8,128)(2,1)S(1)} collective-permute-done((bf16[2,2,256,768]{3,2,1,0:T(8,128)(2,1)S(1)}, bf16[2,2,256,768]{3,2,1,0:T(8,128)(2,1)S(1)}, u32[]{:S(2)}, u32[]{:S(2)}) %collective-permute-start.4) | collective-permute-done | bytes 1572896 | tf_op jit(solution)/shard_map/ppermute | solution.py:20
  422.5 3.9 collective-permute-start.7
  426.4 10.0 %gather_fusion.11 = bf16[9,2,2,256,768]{4,3,2,1,0:T(8,128)(2,1)} fusion(bf16[2,2,5,256,768]{4,3,2,1,0:T(8,128)(2,1)} %bitcast.86, s32[1024]{0:T(1024)S(1)} %get-tuple-element.25), kind=kCustom, calls=%fused_computation.8.clone | custom fusion | bytes 28311588 | tf_op jit(solution)/shard_map/jit(_take)/gather | solution.py:59
  436.4 7.0 %broadcast_select_fusion.2 = bf16[9,2,2,256,768]{4,3,2,1,0:T(8,128)(2,1)S(1)} fusion(bf16[9,2,2,256,768]{4,3,2,1,0:T(8,128)(2,1)} %gather_fusion.11, pred[9]{0:T(512)(128)(4,1)S(1)} %compare_and_fusion.3), kind=kLoop, calls=%fused_computation.14 | loop fusion | flops 7077888 | bytes 28311560 | tf_op jit(solution)/shard_map/jit(_take)/select_n | solution.py:59
  443.4 5.2 convolution_bitcast_fusion
  448.6 4.8 copy.48
  453.4 9.6 %copy.49 = f32[2,2,768,768]{2,3,1,0:T(8,128)} copy(f32[2,2,768,768]{3,2,1,0:T(8,128)} %bitcast.89) | data formatting | bytes 18874368 | tf_op jit(solution)/shard_map/reshape | solution.py:63
  463.0 19.5 %collective-permute-done.6 = bf16[2,2,1280,256]{3,2,1,0:T(8,128)(2,1)} collective-permute-done((bf16[2,2,1280,256]{3,2,1,0:T(8,128)(2,1)}, bf16[2,2,1280,256]{3,2,1,0:T(8,128)(2,1)}, u32[]{:S(2)}, u32[]{:S(2)}) %collective-permute-start.6) | collective-permute-done | bytes 2621472 | tf_op jit(solution)/shard_map/ppermute | solution.py:20
  482.5 6.7 %pad_maximum_fusion = bf16[2,2,768,1280]{3,2,1,0:T(8,128)(2,1)} fusion(bf16[2,2,1280,256]{3,2,1,0:T(8,128)(2,1)} %collective-permute-done.7, bf16[2,2,1280,256]{3,2,1,0:T(8,128)(2,1)} %collective-permute-done.6, bf16[2,2,256,768]{3,2,1,0:T(8,128)(2,1)} %copy-done.5, bf16[2,2,768,768]{3,2,1,0:T(8,128)(2,1)} %fusion.1, ...), kind=kLoop, calls=%fused_computation.20 | loop fusion | flops 39321600 | bytes 20971520 | tf_op jit(solution)/shard_map/concatenate | solution.py:24
  489.2 10.7 %copy.41 = bf16[2,2,768,1280]{2,3,1,0:T(8,128)(2,1)} copy(bf16[2,2,768,1280]{3,2,1,0:T(8,128)(2,1)} %pad_maximum_fusion) | data formatting | bytes 15728640 | tf_op jit(solution)/shard_map/slice | solution.py:117
  499.9 7.1 %copy.42 = bf16[2,2,768,5,256]{2,4,1,0,3:T(8,128)(2,1)} copy(bf16[2,2,768,5,256]{2,4,3,1,0:T(8,128)(2,1)} %bitcast.91) | data formatting | bytes 15728640 | tf_op jit(solution)/shard_map/reshape | solution.py:69
  507.0 10.0 %gather_fusion.10 = bf16[9,2,2,768,256]{3,4,2,1,0:T(8,128)(2,1)} fusion(bf16[2,2,768,5,256]{2,4,1,0,3:T(8,128)(2,1)} %copy.42, s32[1024]{0:T(1024)S(1)} %pad_clamp_fusion), kind=kCustom, calls=%fused_computation.11.clone | custom fusion | bytes 28311588 | tf_op jit(solution)/shard_map/jit(_take)/gather | solution.py:71
  517.0 7.1 %broadcast_select_fusion.1 = bf16[9,2,2,768,256]{3,4,2,1,0:T(8,128)(2,1)S(1)} fusion(bf16[9,2,2,768,256]{3,4,2,1,0:T(8,128)(2,1)} %gather_fusion.10, pred[9]{0:T(512)(128)(4,1)S(1)} %compare_and_fusion), kind=kLoop, calls=%fused_computation.13 | loop fusion | flops 7077888 | bytes 28311560 | tf_op jit(solution)/shard_map/jit(_take)/select_n | solution.py:71
  527.9 4.8 copy.45
  532.8 10.2 %fusion = bf16[2,2,768,768]{2,3,1,0:T(8,128)(2,1)} fusion(f32[2,2,768,768]{2,3,1,0:T(8,128)} %copy.49, f32[2,2,768,3,256]{2,4,3,1,0:T(8,128)} %copy.45), kind=kLoop, calls=%fused_computation.17 | loop fusion | flops 4718592 | bytes 23592960 | tf_op jit(solution)/shard_map/convert_element_type | solution.py:125
  542.9 6.6 %copy.50 = bf16[2,2,768,768]{3,2,1,0:T(8,128)(2,1)} copy(bf16[2,2,768,768]{2,3,1,0:T(8,128)(2,1)} %fusion) | data formatting | bytes 9437184 | tf_op jit(solution)/shard_map/convert_element_type | solution.py:125
  (88 shorter events, 50.5 us)
Async XLA Ops:
  6.5 12.7 %copy-start = (s32[48]{0:T(128)S(1)}, s32[48]{0:T(128)}, u32[]{:S(2)}) copy-start(s32[48]{0:T(128)} %param.20) | copy-start | bytes 580
  6.5 9.6 %copy-start.9 = (s32[48,3]{0,1:T(4,128)S(1)}, s32[48,3]{0,1:T(4,128)}, u32[]{:S(2)}) copy-start(s32[48,3]{0,1:T(4,128)} %param.19) | copy-start | bytes 1732
  6.5 11.3 %copy-start.8 = (f32[12288]{0:T(1024)S(1)}, f32[12288]{0:T(1024)}, u32[]{:S(2)}) copy-start(f32[12288]{0:T(1024)} %param.21) | copy-start | bytes 147460
  6.5 223.0 %all-reduce.2.cloned.1.call-start = ((), (), s32[]{:S(2)}) async-start(), calls=%async_computation | async-start | bytes 2359296 | tf_op jit(solution)/shard_map/psum | solution.py:12
  11.5 98.8 %collective-permute-start.1 = (bf16[2,2,256,768]{3,2,1,0:T(8,128)(2,1)}, bf16[2,2,256,768]{3,2,1,0:T(8,128)(2,1)S(1)}, u32[]{:S(2)}, u32[]{:S(2)}) collective-permute-start(bf16[2,2,256,768]{3,2,1,0:T(8,128)(2,1)} %get-tuple-element.21), channel_id=1, source_target_pairs={{16,0},{32,16},{48,32},{64,48},{80,64},{96,80},{112,96},{128,112},... | collective-permute-start | bytes 4718600 | tf_op jit(solution)/shard_map/ppermute | solution.py:23
  14.1 92.0 %collective-permute-start = (bf16[2,2,256,768]{3,2,1,0:T(8,128)(2,1)}, bf16[2,2,256,768]{3,2,1,0:T(8,128)(2,1)}, u32[]{:S(2)}, u32[]{:S(2)}) collective-permute-start(bf16[2,2,256,768]{3,2,1,0:T(8,128)(2,1)} %get-tuple-element.22), channel_id=1, source_target_pairs={{0,16},{16,32},{32,48},{48,64},{64,80},{80,96},{96,112},{112,128},... | collective-permute-start | bytes 4718600 | tf_op jit(solution)/shard_map/ppermute | solution.py:20
  110.5 13.4 %copy-start.3 = (bf16[2,2,1280,768]{3,2,1,0:T(8,128)(2,1)}, bf16[2,2,1280,768]{3,2,1,0:T(8,128)(2,1)S(1)}, u32[]{:S(2)}) copy-start(bf16[2,2,1280,768]{3,2,1,0:T(8,128)(2,1)S(1)} %constant_dynamic-update-slice_fusion) | copy-start | bytes 23592964
  113.4 130.0 %collective-permute-start.2 = (bf16[2,2,1280,256]{3,2,1,0:T(8,128)(2,1)}, bf16[2,2,1280,256]{3,2,1,0:T(8,128)(2,1)}, u32[]{:S(2)}, u32[]{:S(2)}) collective-permute-start(bf16[2,2,1280,256]{3,2,1,0:T(8,128)(2,1)} %get-tuple-element.17), channel_id=1, source_target_pairs={{0,1},{1,2},{2,3},{3,4},{4,5},{5,6},{6,7},{7,8},{8,9},{9,10},{10,1... | collective-permute-start | bytes 7864328 | tf_op jit(solution)/shard_map/ppermute | solution.py:20
  116.8 126.6 %collective-permute-start.3 = (bf16[2,2,1280,256]{3,2,1,0:T(8,128)(2,1)}, bf16[2,2,1280,256]{3,2,1,0:T(8,128)(2,1)}, u32[]{:S(2)}, u32[]{:S(2)}) collective-permute-start(bf16[2,2,1280,256]{3,2,1,0:T(8,128)(2,1)} %get-tuple-element.18), channel_id=1, source_target_pairs={{1,0},{2,1},{3,2},{4,3},{5,4},{6,5},{7,6},{8,7},{9,8},{10,9},{11,1... | collective-permute-start | bytes 7864328 | tf_op jit(solution)/shard_map/ppermute | solution.py:23
  277.8 7.1 %copy-start.6 = (bf16[3,3,256,256]{3,2,1,0:T(8,128)(2,1)S(1)}, bf16[3,3,256,256]{3,2,1,0:T(8,128)(2,1)}, u32[]{:S(2)}) copy-start(bf16[3,3,256,256]{3,2,1,0:T(8,128)(2,1)} %param.18) | copy-start | bytes 3538948
  313.9 100.3 %copy-start.4 = (bf16[2,2,768,768]{3,2,1,0:T(8,128)(2,1)S(1)}, bf16[2,2,768,768]{3,2,1,0:T(8,128)(2,1)}, u32[]{:S(2)}) copy-start(bf16[2,2,768,768]{3,2,1,0:T(8,128)(2,1)} %fusion.1) | copy-start | bytes 14155780
  316.2 96.9 %collective-permute-start.4 = (bf16[2,2,256,768]{3,2,1,0:T(8,128)(2,1)S(1)}, bf16[2,2,256,768]{3,2,1,0:T(8,128)(2,1)S(1)}, u32[]{:S(2)}, u32[]{:S(2)}) collective-permute-start(bf16[2,2,256,768]{3,2,1,0:T(8,128)(2,1)S(1)} %get-tuple-element.19), channel_id=1, source_target_pairs={{0,16},{16,32},{32,48},{48,64},{64,80},{80,96},{96,112},{112,128},... | collective-permute-start | bytes 4718600 | tf_op jit(solution)/shard_map/ppermute | solution.py:20
  318.2 94.9 %collective-permute-start.5 = (bf16[2,2,256,768]{3,2,1,0:T(8,128)(2,1)S(1)}, bf16[2,2,256,768]{3,2,1,0:T(8,128)(2,1)S(1)}, u32[]{:S(2)}, u32[]{:S(2)}) collective-permute-start(bf16[2,2,256,768]{3,2,1,0:T(8,128)(2,1)S(1)} %get-tuple-element.20), channel_id=1, source_target_pairs={{16,0},{32,16},{48,32},{64,48},{80,64},{96,80},{112,96},{128,112},... | collective-permute-start | bytes 4718600 | tf_op jit(solution)/shard_map/ppermute | solution.py:23
  413.1 1.1 copy-start.5
  414.8 3.1 copy-start.2
  420.6 61.9 %collective-permute-start.6 = (bf16[2,2,1280,256]{3,2,1,0:T(8,128)(2,1)}, bf16[2,2,1280,256]{3,2,1,0:T(8,128)(2,1)}, u32[]{:S(2)}, u32[]{:S(2)}) collective-permute-start(bf16[2,2,1280,256]{3,2,1,0:T(8,128)(2,1)} %get-tuple-element.14), channel_id=1, source_target_pairs={{0,1},{1,2},{2,3},{3,4},{4,5},{5,6},{6,7},{7,8},{8,9},{9,10},{10,1... | collective-permute-start | bytes 7864328 | tf_op jit(solution)/shard_map/ppermute | solution.py:20
  422.5 60.0 %collective-permute-start.7 = (bf16[2,2,1280,256]{3,2,1,0:T(8,128)(2,1)}, bf16[2,2,1280,256]{3,2,1,0:T(8,128)(2,1)}, u32[]{:S(2)}, u32[]{:S(2)}) collective-permute-start(bf16[2,2,1280,256]{3,2,1,0:T(8,128)(2,1)} %get-tuple-element.16), channel_id=1, source_target_pairs={{1,0},{2,1},{3,2},{4,3},{5,4},{6,5},{7,6},{8,7},{9,8},{10,9},{11,1... | collective-permute-start | bytes 7864328 | tf_op jit(solution)/shard_map/ppermute | solution.py:23
  517.0 7.1 %copy-start.7 = (bf16[3,3,256,256]{3,2,1,0:T(8,128)(2,1)S(1)}, bf16[3,3,256,256]{3,2,1,0:T(8,128)(2,1)}, u32[]{:S(2)}) copy-start(bf16[3,3,256,256]{3,2,1,0:T(8,128)(2,1)} %param.18) | copy-start | bytes 3538948
  532.8 16.8 %copy-start.1 = (s32[48]{0:T(128)S(1)}, s32[48]{0:T(128)}, u32[]{:S(2)}) copy-start(s32[48]{0:T(128)} %param.20) | copy-start | bytes 580
Sparse Core Ops, SparseCore 0:
  10.0 219.4 all-reduce.1
where the time goes:
time: 558 us; the launch traced here: 556 us
  waiting for transfers between devices  278 us (50%)
  local copies, waits for them, and re-layouts  149 us (27%)
  other arithmetic  67.9 us (12%)
  starting transfers between devices  24.3 us (4%)
  matrix products  22.6 us (4%)
  between operations  13.8 us (2%)
    ppermute x4, waiting for transfers between devices, with_halo(): lax.ppermute(lax.slice_in_dim(block, block.shape[dim] - width, None, axis...  193 us
    psum x1, waiting for transfers between devices, broadcast(): return lax.psum(kept, axis)  84.9 us
    gather x2, local copies, waits for them, and re-layouts, left_apply(): jnp.take(pieces, relative, axis=2)  20 us
    gather x2, local copies, waits for them, and re-layouts, right_apply(): jnp.take(pieces, relative, axis=3)  20 us
    select_n x3, other arithmetic, left_apply(): jnp.take(pieces, relative, axis=2)  17.7 us
    ppermute x4, starting transfers between devices, with_halo(): lax.ppermute(lax.slice_in_dim(block, 0, width, axis=dim), axis, backward)  15 us
    dot_general x2, matrix products, left_apply(): jnp.einsum('ikab,rpikbc->rpiac', matrix, picked, preferred_element_type=j...  14.3 us
    reshape x2, local copies, waits for them, and re-layouts, right_apply(): source_operator.reshape(copies, halves, source_rows, breadth // block_siz...  14.1 us
  transfers between devices with their start and end apart: 9, of which 4 were waited for; matrix products, arithmetic and copies ran while one was open for 16% of the time, Pallas kernels for 0%

commit v1 on v0

--- a/solution.py
+++ b/solution.py
@@ -9,7 +9,7 @@
 
 def broadcast(value, axis, source):
     kept = jnp.where(lax.axis_index(axis) == source, value, 0).astype(value.dtype)
-    return lax.psum(kept, axis)
+    return jnp.sum(lax.all_gather(kept, axis), axis=0)
 
 
 def with_halo(block, sides, width):

time: 558 us -> 830 us (1.49)
  the two profiles are of different devices: /device:TPU:92 before, /device:TPU:45 now
where the time goes in v1:
time: 830 us; the launch traced here: 828 us
  waiting for transfers between devices  542 us (65%)
  local copies, waits for them, and re-layouts  150 us (18%)
  other arithmetic  77 us (9%)
  matrix products  23 us (3%)
  starting transfers between devices  22.6 us (3%)
  between operations  13.8 us (2%)
    ppermute x4, waiting for transfers between devices, with_halo(): lax.ppermute(lax.slice_in_dim(block, block.shape[dim] - width, None, axis...  352 us
    all_gather x1, waiting for transfers between devices, broadcast(): return jnp.sum(lax.all_gather(kept, axis), axis=0)  126 us
    ppermute x4, waiting for transfers between devices, with_halo(): lax.ppermute(lax.slice_in_dim(block, 0, width, axis=dim), axis, backward)  65.1 us
    gather x2, local copies, waits for them, and re-layouts, right_apply(): jnp.take(pieces, relative, axis=3)  20.3 us
    gather x2, local copies, waits for them, and re-layouts, left_apply(): jnp.take(pieces, relative, axis=2)  20 us
    select_n x3, other arithmetic, left_apply(): jnp.take(pieces, relative, axis=2)  17.9 us
  transfers between devices with their start and end apart: 9, of which 6 were waited for; matrix products, arithmetic and copies ran while one was open for 17% of the time, Pallas kernels for 0%

profile of v1, /device:TPU:45, one launch (start us, length us, event | category | flops | bytes accessed | tf_op | source)
XLA Modules:
  0.0 828.3 jit_solution(10584637982654994003)
XLA Ops:
  24.3 145.8 %collective-permute-done = bf16[2,2,256,768]{3,2,1,0:T(8,128)(2,1)} collective-permute-done((bf16[2,2,256,768]{3,2,1,0:T(8,128)(2,1)}, bf16[2,2,256,768]{3,2,1,0:T(8,128)(2,1)}, u32[]{:S(2)}, u32[]{:S(2)}) %collective-permute-start) | collective-permute-done | bytes 1572896 | tf_op jit(solution)/shard_map/ppermute | solution.py:20
  186.6 10.0 %gather_fusion.2 = bf16[9,2,2,256,768]{4,3,2,1,0:T(8,128)(2,1)} fusion(bf16[2,2,5,256,768]{4,3,1,0,2:T(8,128)(2,1)} %copy.53, s32[1024]{0:T(1024)S(1)} %get-tuple-element.25), kind=kCustom, calls=%fused_computation.2.clone | custom fusion | bytes 28311588 | tf_op jit(solution)/shard_map/jit(_take)/gather | solution.py:59
  196.6 10.9 %broadcast_select_fusion.3 = bf16[9,2,2,256,768]{4,3,2,1,0:T(8,128)(2,1)} fusion(bf16[9,2,2,256,768]{4,3,2,1,0:T(8,128)(2,1)} %gather_fusion.2, pred[9]{0:T(512)(128)(4,1)S(1)} %compare_and_fusion.3), kind=kLoop, calls=%fused_computation.15 | loop fusion | flops 7077888 | bytes 28311560 | tf_op jit(solution)/shard_map/jit(_take)/select_n | solution.py:59
  207.5 154.7 %collective-permute-done.2 = bf16[2,2,1280,256]{3,2,1,0:T(8,128)(2,1)} collective-permute-done((bf16[2,2,1280,256]{3,2,1,0:T(8,128)(2,1)}, bf16[2,2,1280,256]{3,2,1,0:T(8,128)(2,1)}, u32[]{:S(2)}, u32[]{:S(2)}) %collective-permute-start.2) | collective-permute-done | bytes 2621472 | tf_op jit(solution)/shard_map/ppermute | solution.py:20
  362.2 5.5 pad_maximum_fusion.4
  367.8 10.6 %copy.57 = bf16[2,2,768,1280]{2,3,1,0:T(8,128)(2,1)} copy(bf16[2,2,768,1280]{3,2,1,0:T(8,128)(2,1)} %pad_maximum_fusion.4) | data formatting | bytes 15728640 | tf_op jit(solution)/shard_map/slice | solution.py:108
  378.4 7.1 copy.58
  385.5 10.1 %gather_fusion.9 = bf16[9,2,2,768,256]{3,4,2,1,0:T(8,128)(2,1)} fusion(bf16[2,2,768,5,256]{2,4,1,0,3:T(8,128)(2,1)} %copy.58, s32[1024]{0:T(1024)S(1)} %pad_clamp_fusion), kind=kCustom, calls=%fused_computation.5.clone | custom fusion | bytes 28311588 | tf_op jit(solution)/shard_map/jit(_take)/gather | solution.py:71
  395.6 7.1 broadcast_select_fusion
  407.2 4.8 copy.61
  412.0 9.6 %copy.62 = f32[2,2,768,768]{3,2,1,0:T(8,128)} copy(f32[2,2,768,768]{2,3,1,0:T(8,128)} %bitcast.89) | data formatting | bytes 18874368 | tf_op jit(solution)/shard_map/reshape | solution.py:75
  421.6 125.6 %all-gather.3.cloned.1.call-done = bf16[48,3,256,256]{3,2,1,0:T(8,128)(2,1)} async-done(((bf16[3,3,256,256]{3,2,1,0:T(8,128)(2,1)}), bf16[48,3,256,256]{3,2,1,0:T(8,128)(2,1)}) %all-gather.3.cloned.1.call-update) | async-done | bytes 18874384 | tf_op jit(solution)/shard_map/all_gather | solution.py:12
  547.2 10.2 %reduce_sum.12 = bf16[3,3,256,256]{3,2,1,0:T(8,128)(2,1)S(1)} reduce(bf16[16,3,3,256,256]{4,3,2,1,0:T(8,128)(2,1)} %bitcast.93, bf16[]{:T(256)} %constant.78.clone.1), dimensions={0}, to_apply=%region_0.0 | reduce | flops 8847360 | bytes 20054018 | tf_op jit(solution)/shard_map/reduce_sum | solution.py:12
  557.4 9.5 %convolution_bitcast_fusion.3 = f32[2,2,3,256,768]{4,3,1,0,2:T(8,128)S(1)} fusion(bf16[2,2,3,3,256,768]{5,4,1,0,3,2:T(8,128)(2,1)} %bitcast.94, bf16[3,3,256,256]{3,2,1,0:T(8,128)(2,1)S(1)} %reduce_sum.12, f32[3,3,256]{2,1,0:T(4,128)S(1)} %sub.69, f32[3,256]{1,0:T(4,128)S(1)} %broadcast_select_fusion.8, pred[3,3]{1,0:T(4,128)(4,1)S(1)} %fusion.47), kind=kOutput, calls=%fused_computation.30 | convolution fusion | flops 3630956544 | bytes 24784904 | tf_op jit(solution)/shard_map/ikab,rpikbc->rpiac/dot_general | solution.py:62
  566.9 4.8 copy.56
  571.7 10.1 %fusion.1 = bf16[2,2,768,768]{3,2,1,0:T(8,128)(2,1)} fusion(f32[2,2,768,768]{3,2,1,0:T(8,128)} %copy.62, f32[2,2,3,256,768]{4,3,2,1,0:T(8,128)} %copy.56), kind=kLoop, calls=%fused_computation.19 | loop fusion | flops 4718592 | bytes 23592960 | tf_op jit(solution)/shard_map/convert_element_type | solution.py:110
  588.8 32.2 %collective-permute-done.4 = bf16[2,2,256,768]{3,2,1,0:T(8,128)(2,1)S(1)} collective-permute-done((bf16[2,2,256,768]{3,2,1,0:T(8,128)(2,1)S(1)}, bf16[2,2,256,768]{3,2,1,0:T(8,128)(2,1)S(1)}, u32[]{:S(2)}, u32[]{:S(2)}) %collective-permute-start.4) | collective-permute-done | bytes 1572896 | tf_op jit(solution)/shard_map/ppermute | solution.py:20
  621.0 65.1 %collective-permute-done.5 = bf16[2,2,256,768]{3,2,1,0:T(8,128)(2,1)S(1)} collective-permute-done((bf16[2,2,256,768]{3,2,1,0:T(8,128)(2,1)S(1)}, bf16[2,2,256,768]{3,2,1,0:T(8,128)(2,1)S(1)}, u32[]{:S(2)}, u32[]{:S(2)}) %collective-permute-start.5) | collective-permute-done | bytes 1572896 | tf_op jit(solution)/shard_map/ppermute | solution.py:23
  698.8 10.0 %gather_fusion.11 = bf16[9,2,2,256,768]{4,3,2,1,0:T(8,128)(2,1)} fusion(bf16[2,2,5,256,768]{4,3,2,1,0:T(8,128)(2,1)} %bitcast.87, s32[1024]{0:T(1024)S(1)} %get-tuple-element.25), kind=kCustom, calls=%fused_computation.8.clone | custom fusion | bytes 28311588 | tf_op jit(solution)/shard_map/jit(_take)/gather | solution.py:59
  708.8 7.0 broadcast_select_fusion.2
  715.8 5.2 convolution_bitcast_fusion
  721.0 4.8 copy.70
  725.8 9.7 %copy.71 = f32[2,2,768,768]{2,3,1,0:T(8,128)} copy(f32[2,2,768,768]{3,2,1,0:T(8,128)} %bitcast.90) | data formatting | bytes 18874368 | tf_op jit(solution)/shard_map/reshape | solution.py:63
  735.4 18.9 %collective-permute-done.6 = bf16[2,2,1280,256]{3,2,1,0:T(8,128)(2,1)} collective-permute-done((bf16[2,2,1280,256]{3,2,1,0:T(8,128)(2,1)}, bf16[2,2,1280,256]{3,2,1,0:T(8,128)(2,1)}, u32[]{:S(2)}, u32[]{:S(2)}) %collective-permute-start.6) | collective-permute-done | bytes 2621472 | tf_op jit(solution)/shard_map/ppermute | solution.py:20
  754.3 6.8 pad_maximum_fusion
  761.2 10.6 %copy.63 = bf16[2,2,768,1280]{2,3,1,0:T(8,128)(2,1)} copy(bf16[2,2,768,1280]{3,2,1,0:T(8,128)(2,1)} %pad_maximum_fusion) | data formatting | bytes 15728640 | tf_op jit(solution)/shard_map/slice | solution.py:117
  771.8 7.1 copy.64
  778.9 10.2 %gather_fusion.10 = bf16[9,2,2,768,256]{3,4,2,1,0:T(8,128)(2,1)} fusion(bf16[2,2,768,5,256]{2,4,1,0,3:T(8,128)(2,1)} %copy.64, s32[1024]{0:T(1024)} %copy-done.11), kind=kCustom, calls=%fused_computation.11.clone | custom fusion | bytes 28311588 | tf_op jit(solution)/shard_map/jit(_take)/gather | solution.py:71
  789.1 7.1 broadcast_select_fusion.1
  800.0 4.8 copy.67
  804.8 10.1 %fusion = bf16[2,2,768,768]{2,3,1,0:T(8,128)(2,1)} fusion(f32[2,2,768,768]{2,3,1,0:T(8,128)} %copy.71, f32[2,2,768,3,256]{2,4,3,1,0:T(8,128)} %copy.67), kind=kLoop, calls=%fused_computation.17 | loop fusion | flops 4718592 | bytes 23592960 | tf_op jit(solution)/shard_map/convert_element_type | solution.py:125
  814.8 6.6 copy.72
  (99 shorter events, 62.2 us)
Async XLA Ops:
  6.5 12.0 %copy-start = (s32[48]{0:T(128)S(1)}, s32[48]{0:T(128)}, u32[]{:S(2)}) copy-start(s32[48]{0:T(128)} %param.20) | copy-start | bytes 580
  6.5 13.4 %copy-start.12 = (s32[48,3]{0,1:T(4,128)S(1)}, s32[48,3]{0,1:T(4,128)}, u32[]{:S(2)}) copy-start(s32[48,3]{0,1:T(4,128)} %param.19) | copy-start | bytes 1732
  6.5 14.6 %copy-start.10 = (f32[12288]{0:T(1024)S(1)}, f32[12288]{0:T(1024)}, u32[]{:S(2)}) copy-start(f32[12288]{0:T(1024)} %param.21) | copy-start | bytes 147460
  6.5 540.7 %all-gather.3.cloned.1.call-start = ((), (), s32[]{:S(2)}) async-start(), calls=%async_computation | async-start | bytes 20054016 | tf_op jit(solution)/shard_map/all_gather | solution.py:12
  11.5 162.8 %collective-permute-start.1 = (bf16[2,2,256,768]{3,2,1,0:T(8,128)(2,1)}, bf16[2,2,256,768]{3,2,1,0:T(8,128)(2,1)S(1)}, u32[]{:S(2)}, u32[]{:S(2)}) collective-permute-start(bf16[2,2,256,768]{3,2,1,0:T(8,128)(2,1)} %get-tuple-element.21), channel_id=1, source_target_pairs={{16,0},{32,16},{48,32},{64,48},{80,64},{96,80},{112,96},{128,112},... | collective-permute-start | bytes 4718600 | tf_op jit(solution)/shard_map/ppermute | solution.py:23
  14.1 156.0 %collective-permute-start = (bf16[2,2,256,768]{3,2,1,0:T(8,128)(2,1)}, bf16[2,2,256,768]{3,2,1,0:T(8,128)(2,1)}, u32[]{:S(2)}, u32[]{:S(2)}) collective-permute-start(bf16[2,2,256,768]{3,2,1,0:T(8,128)(2,1)} %get-tuple-element.22), channel_id=1, source_target_pairs={{0,16},{16,32},{32,48},{48,64},{64,80},{80,96},{96,112},{112,128},... | collective-permute-start | bytes 4718600 | tf_op jit(solution)/shard_map/ppermute | solution.py:20
  24.2 361.3 %copy-start.11 = (s32[1024]{0:T(1024)}, s32[1024]{0:T(1024)S(1)}, u32[]{:S(2)}) copy-start(s32[1024]{0:T(1024)S(1)} %pad_clamp_fusion) | copy-start | bytes 12292
  24.2 371.4 %copy-start.13 = (pred[9]{0:T(512)(128)(4,1)}, pred[9]{0:T(512)(128)(4,1)S(1)}, u32[]{:S(2)}) copy-start(pred[9]{0:T(512)(128)(4,1)S(1)} %compare_and_fusion) | copy-start | bytes 31
  174.4 12.3 %copy-start.3 = (bf16[2,2,1280,768]{3,2,1,0:T(8,128)(2,1)}, bf16[2,2,1280,768]{3,2,1,0:T(8,128)(2,1)S(1)}, u32[]{:S(2)}) copy-start(bf16[2,2,1280,768]{3,2,1,0:T(8,128)(2,1)S(1)} %constant_dynamic-update-slice_fusion) | copy-start | bytes 23592964
  177.3 185.0 %collective-permute-start.2 = (bf16[2,2,1280,256]{3,2,1,0:T(8,128)(2,1)}, bf16[2,2,1280,256]{3,2,1,0:T(8,128)(2,1)}, u32[]{:S(2)}, u32[]{:S(2)}) collective-permute-start(bf16[2,2,1280,256]{3,2,1,0:T(8,128)(2,1)} %get-tuple-element.17), channel_id=1, source_target_pairs={{0,1},{1,2},{2,3},{3,4},{4,5},{5,6},{6,7},{7,8},{8,9},{9,10},{10,1... | collective-permute-start | bytes 7864328 | tf_op jit(solution)/shard_map/ppermute | solution.py:20
  179.2 183.0 %collective-permute-start.3 = (bf16[2,2,1280,256]{3,2,1,0:T(8,128)(2,1)}, bf16[2,2,1280,256]{3,2,1,0:T(8,128)(2,1)}, u32[]{:S(2)}, u32[]{:S(2)}) collective-permute-start(bf16[2,2,1280,256]{3,2,1,0:T(8,128)(2,1)} %get-tuple-element.18), channel_id=1, source_target_pairs={{1,0},{2,1},{3,2},{4,3},{5,4},{6,5},{7,6},{8,7},{9,8},{10,9},{11,1... | collective-permute-start | bytes 7864328 | tf_op jit(solution)/shard_map/ppermute | solution.py:23
  196.6 165.6 %copy-start.4 = (bf16[2,2,1280,768]{3,2,1,0:T(8,128)(2,1)S(1)}, bf16[2,2,1280,768]{3,2,1,0:T(8,128)(2,1)}, u32[]{:S(2)}) copy-start(bf16[2,2,1280,768]{3,2,1,0:T(8,128)(2,1)} %copy-done.3) | copy-start | bytes 23592964
  395.6 7.1 copy-start.8
  557.4 9.5 %copy-start.7 = (bf16[3,3,256,256]{3,2,1,0:T(8,128)(2,1)}, bf16[3,3,256,256]{3,2,1,0:T(8,128)(2,1)S(1)}, u32[]{:S(2)}) copy-start(bf16[3,3,256,256]{3,2,1,0:T(8,128)(2,1)S(1)} %reduce_sum.12) | copy-start | bytes 3538948
  581.7 105.5 %copy-start.5 = (bf16[2,2,768,768]{3,2,1,0:T(8,128)(2,1)S(1)}, bf16[2,2,768,768]{3,2,1,0:T(8,128)(2,1)}, u32[]{:S(2)}) copy-start(bf16[2,2,768,768]{3,2,1,0:T(8,128)(2,1)} %fusion.1) | copy-start | bytes 14155780
  584.0 37.0 %collective-permute-start.4 = (bf16[2,2,256,768]{3,2,1,0:T(8,128)(2,1)S(1)}, bf16[2,2,256,768]{3,2,1,0:T(8,128)(2,1)S(1)}, u32[]{:S(2)}, u32[]{:S(2)}) collective-permute-start(bf16[2,2,256,768]{3,2,1,0:T(8,128)(2,1)S(1)} %get-tuple-element.19), channel_id=1, source_target_pairs={{0,16},{16,32},{32,48},{48,64},{64,80},{80,96},{96,112},{112,128},... | collective-permute-start | bytes 4718600 | tf_op jit(solution)/shard_map/ppermute | solution.py:20
  586.8 99.3 %collective-permute-start.5 = (bf16[2,2,256,768]{3,2,1,0:T(8,128)(2,1)S(1)}, bf16[2,2,256,768]{3,2,1,0:T(8,128)(2,1)S(1)}, u32[]{:S(2)}, u32[]{:S(2)}) collective-permute-start(bf16[2,2,256,768]{3,2,1,0:T(8,128)(2,1)S(1)} %get-tuple-element.20), channel_id=1, source_target_pairs={{16,0},{32,16},{48,32},{64,48},{80,64},{96,80},{112,96},{128,112},... | collective-permute-start | bytes 4718600 | tf_op jit(solution)/shard_map/ppermute | solution.py:23
  686.1 1.2 copy-start.6
  687.8 3.1 copy-start.2
  693.6 60.8 %collective-permute-start.6 = (bf16[2,2,1280,256]{3,2,1,0:T(8,128)(2,1)}, bf16[2,2,1280,256]{3,2,1,0:T(8,128)(2,1)}, u32[]{:S(2)}, u32[]{:S(2)}) collective-permute-start(bf16[2,2,1280,256]{3,2,1,0:T(8,128)(2,1)} %get-tuple-element.14), channel_id=1, source_target_pairs={{0,1},{1,2},{2,3},{3,4},{4,5},{5,6},{6,7},{7,8},{8,9},{9,10},{10,1... | collective-permute-start | bytes 7864328 | tf_op jit(solution)/shard_map/ppermute | solution.py:20
  695.5 58.9 %collective-permute-start.7 = (bf16[2,2,1280,256]{3,2,1,0:T(8,128)(2,1)}, bf16[2,2,1280,256]{3,2,1,0:T(8,128)(2,1)}, u32[]{:S(2)}, u32[]{:S(2)}) collective-permute-start(bf16[2,2,1280,256]{3,2,1,0:T(8,128)(2,1)} %get-tuple-element.16), channel_id=1, source_target_pairs={{1,0},{2,1},{3,2},{4,3},{5,4},{6,5},{7,6},{8,7},{9,8},{10,9},{11,1... | collective-permute-start | bytes 7864328 | tf_op jit(solution)/shard_map/ppermute | solution.py:23
  778.9 10.2 %copy-start.14 = (pred[9]{0:T(512)(128)(4,1)S(1)}, pred[9]{0:T(512)(128)(4,1)}, u32[]{:S(2)}) copy-start(pred[9]{0:T(512)(128)(4,1)} %copy-done.13) | copy-start | bytes 31
  789.1 7.1 copy-start.9
  804.8 16.7 %copy-start.1 = (s32[48]{0:T(128)S(1)}, s32[48]{0:T(128)}, u32[]{:S(2)}) copy-start(s32[48]{0:T(128)} %param.20) | copy-start | bytes 580
Sparse Core Ops, SparseCore 0:
  9.2 538.0 all-gather.2
